TPU v7x, 32 devices: a whole 2x2x4 slice. The times are simulated.
32 devices in a mesh: groups: 2 (over y), section: 4 (over z), head: 4 (over x, core).
Axes of the slice: x: 2, y: 2, z: 4, core: 2. Of those that a mesh axis runs over, the one named last changes fastest.
Arguments:
- rising: bfloat16 [8, 128, 1024], P(('groups', 'section')), parts along dimension 0, may hold values from -24 to 24
- falling: bfloat16 [8, 128, 1024], P(('groups', 'section')), parts along dimension 0, may hold values from -6 to 6
- stash: bfloat16 [8, 3, 128, 1024], P(('groups', 'section')), parts along dimension 0, may hold values from -24 to 24
- queue: bfloat16 [12, 128, 1024], P('groups'), parts along dimension 0, may hold values from -24 to 24
- order: int32 [12], P('groups'), parts along dimension 0, may hold values from 0 to 5, each once
- buckets: int32 [128, 128], replicated, may hold values from 0 to 31, as said below
- bias_table: float32 [4, 32, 64], P('section', None, 'head'), may hold values from -3 to 260
- gain: float32 [4, 1024], P('section'), may hold values from 0.1 to 1.9
- w_qkv: bfloat16 [4, 1024, 64, 3, 128], P('section', None, 'head'), may hold values from -0.1875 to 0.1875
- w_out: bfloat16 [4, 64, 128, 1024], P('section', 'head'), may hold values from -0.0625 to 0.0625
Outputs:
- rising_out: bfloat16 [8, 128, 1024], P(('groups', 'section')), parts along dimension 0
- falling_out: bfloat16 [8, 128, 1024], P(('groups', 'section')), parts along dimension 0
- table_grad: float32 [8, 32, 64], P(('groups', 'section'), None, 'head'), parts along dimension 0
There are 2 independent parts, one for each index of `groups`. A program takes and returns all parts, laid end to end along the dimension named above; an argument that names none is the same for every part. Nothing has to cross between parts.
Inputs may be any that keep to these rules, and one draw needn't show every extreme that they name: `order`: a permutation of 0 to 5. T5's bidirectional bucket of the key's position minus the query's, 32 buckets, distances of 128 or more in the outermost; positions rise by 1 to 4 from token to token, with one jump of 128 or more.
All inputs are finite; a program needn't handle non-finite values.
Results may differ from a plain program's by a relative error of at most 0.019.
Values may be sent and summed in bfloat16 or wider, within the bound.
A program may use at most 128 MiB of HBM per device.

v0:
```python
import functools

import jax
import jax.numpy as jnp
from jax import lax
from jax.experimental import pallas as pl
from jax.experimental.pallas import tpu as pltpu
from jax.sharding import PartitionSpec as P

EPSILON = 1e-06
MESH = pl.DeviceIdType.MESH
NN = (((1,), (0,)), ((), ()))
NT = (((1,), (1,)), ((), ()))
TN = (((0,), (0,)), ((), ()))


def mm(a, b, dims):
    return lax.dot_general(a, b, dims, preferred_element_type=jnp.float32)


def inverse_rms(x):
    return lax.rsqrt(jnp.mean(x * x, axis=-1, keepdims=True) + EPSILON)


def probabilities(q, k, bias, scale):
    scores = mm(q, k, NT) * scale + bias
    top = jnp.max(scores, axis=-1, keepdims=True)
    raised = jnp.exp(scores - top)
    return raised / jnp.sum(raised, axis=-1, keepdims=True)


def wave_kernel(
    ticks, steps, pair, head_dim, chips, sections,
    order, rising, falling, stash, queue, gain, bias, buckets, w_hbm, wo,
    moved, table,
    w, w_sem, normed, saved, flat_down, acc, total, sums, cur, part, near, away, far, share,
    near_send, near_recv, far_send, far_recv,
    lift_send, lift_recv, gather_send, gather_recv, pass_send, pass_recv,
):
    section = lax.axis_index("section")
    head = lax.axis_index("head")
    chip, core = head // 2, lax.rem(head, 2)
    twin = chip * 2 + (1 - core)
    rows, width = flat_down.shape
    scale = head_dim ** (-0.5)
    span = pair * head_dim

    def peer(k):
        return lax.rem(chip + k, chips)

    def remote(src, dst, send, recv, target):
        return pltpu.make_async_remote_copy(
            src_ref=src, dst_ref=dst, send_sem=send, recv_sem=recv,
            device_id=target, device_id_type=MESH,
        )

    def flat(x):
        return x.astype(jnp.float32).reshape(rows, width)

    def in_block(step, c):
        return w[step, c]

    def load(step, c):
        source = w_hbm.at[:, pl.ds(pl.multiple_of((c * steps + step) * span, 128), span)]
        return pltpu.make_async_copy(source, w.at[step, c], w_sem.at[step, c])

    def out_block(step):
        return wo[pl.ds(pl.multiple_of(step * span, 128), span), :]

    def near_copy(which, t, k):
        return remote(
            part.at[which, t, peer(k), 1 - core], near.at[which, t, k],
            near_send.at[which, t, k], near_recv.at[which, t, k], {"head": twin},
        )

    def far_copy(which, t, k):
        return remote(
            away.at[which, t, k - 1], far.at[which, t, k - 1],
            far_send.at[which, t, k - 1], far_recv.at[which, t, k - 1],
            {"head": peer(k) * 2 + core},
        )

    def lift_copy(which, t, target):
        return remote(
            share.at[which, t], cur.at[which, t + 1, chip, core],
            lift_send.at[which, t], lift_recv.at[which, t], {"section": target},
        )

    def gather_copy(which, t, k):
        rows_here = cur.at[which, t + 1, chip, core]
        return remote(
            rows_here, rows_here,
            gather_send.at[which, t, k - 1], gather_recv.at[which, t, k - 1],
            {"head": peer(k) * 2 + core},
        )

    def pass_copy(which, t, k):
        rows_here = cur.at[which, t + 1, lax.rem(chip - k + chips, chips), core]
        return remote(
            rows_here, rows_here,
            pass_send.at[which, t, k], pass_recv.at[which, t, k], {"head": twin},
        )

    def begin(which, t):
        part[which, t] = acc[...].reshape(part.shape[2:]).astype(jnp.bfloat16)
        for k in list(range(1, chips)) + [0]:
            near_copy(which, t, k).start()

    def fold(which, t):
        for k in range(1, chips):
            near_copy(which, t, k).wait_recv()
            away[which, t, k - 1] = (
                part[which, t, peer(k), core].astype(jnp.float32)
                + near[which, t, k].astype(jnp.float32)
            ).astype(jnp.bfloat16)
            far_copy(which, t, k).start()

    def ends(which):
        if which == 0:
            return section < sections - 1, section + 1, section > 0, section - 1
        return section > 0, section - 1, section < sections - 1, section + 1

    def finish(which, t):
        near_copy(which, t, 0).wait_recv()
        own = part[which, t, chip, core].astype(jnp.float32) + near[which, t, 0].astype(
            jnp.float32
        )
        for k in range(1, chips):
            far_copy(which, t, k).wait_recv()
            own = own + far[which, t, k - 1].astype(jnp.float32)
        before = cur[which, t, chip, core].astype(jnp.float32)
        if which == 0:
            result = before + own
        else:
            x = stash[t, chip, core].astype(jnp.float32)
            inverse = inverse_rms(x)
            cubed = inverse * inverse * inverse
            weighted = gain[...] * own
            result = (
                before
                + inverse * weighted
                - x * cubed * jnp.mean(x * weighted, axis=-1, keepdims=True)
            )
        share[which, t] = result.astype(jnp.bfloat16)
        sends, target, receives, _ = ends(which)

        if t == ticks - 1:
            cur[which, t + 1, chip, core] = result.astype(jnp.bfloat16)
            return

        @pl.when(sends)
        def _():
            lift_copy(which, t, target).start()

        @pl.when(jnp.logical_not(receives))
        def _():
            if which == 0:
                cur[which, t + 1, chip, core] = queue[order[t], chip, core]
            else:
                cur[which, t + 1, chip, core] = share[0, t]

    def spread(which, t):
        sends, target, receives, source = ends(which)

        if t < ticks - 1:
            @pl.when(receives)
            def _():
                lift_copy(which, t, source).wait_recv()

        for k in range(1, chips):
            gather_copy(which, t, k).start()
        pass_copy(which, t, 0).start()

    def relay(which, t):
        for k in range(1, chips):
            gather_copy(which, t, k).wait_recv()
            pass_copy(which, t, k).start()

    def settle(which, t):
        sends, target, receives, source = ends(which)
        relay(which, t)
        for k in range(chips):
            pass_copy(which, t, k).wait_recv()
        for k in range(chips):
            near_copy(which, t, k).wait_send()
            pass_copy(which, t, k).wait_send()
        for k in range(1, chips):
            far_copy(which, t, k).wait_send()
            gather_copy(which, t, k).wait_send()

        if t < ticks - 1:
            @pl.when(sends)
            def _():
                lift_copy(which, t, target).wait_send()

    stages = ((fold, 2), (finish, 4), (spread, 6))

    def normalize(place, x):
        normed[place * rows : (place + 1) * rows, :] = (
            x * inverse_rms(x) * gain[...]
        ).astype(jnp.bfloat16)

    def project(step, count):
        source = normed[: count * rows, :]
        return [mm(source, in_block(step, c), NN).astype(jnp.bfloat16) for c in range(3)]

    def advance(step, which, t):
        for stage, at in stages:
            @pl.when(step == at * steps // 8)
            def _(stage=stage):
                stage(which, t)

    def forward(t):
        def run(step, carry):
            if t > 0:
                advance(step, 1, t - 1)
            if t == 0:
                for c in range(3):
                    load(step, c).wait()
            qkv = project(step, 1 if t > 0 else ticks + 1)
            if t == 0:
                for c in range(3):
                    saved[step, c] = qkv[c][rows:]
            attended = []
            for h in range(pair):
                q, k, v = (a[:rows, h * head_dim : (h + 1) * head_dim] for a in qkv)
                probs = probabilities(q, k, bias[step * pair + h], scale).astype(jnp.bfloat16)
                attended.append(mm(probs, v, NN).astype(jnp.bfloat16))
            acc[...] += mm(jnp.concatenate(attended, axis=1), out_block(step), NN)
            return carry

        lax.fori_loop(0, steps, run, 0)

    def backward(t):
        def run(step, carry):
            advance(step, 0, t)
            grad_flat = mm(flat_down[...], out_block(step), NT).astype(jnp.bfloat16)
            stacked = []
            for h in range(pair):
                columns = slice(h * head_dim, (h + 1) * head_dim)
                q, k, v = (
                    saved[step, c, t * rows : (t + 1) * rows, columns] for c in range(3)
                )
                g = grad_flat[:, columns]
                probs = probabilities(q, k, bias[step * pair + h], scale)
                grad_probs = mm(g, v, NT)
                grad_value = mm(probs.astype(jnp.bfloat16), g, TN).astype(jnp.bfloat16)
                grad_scores = probs * (
                    grad_probs - jnp.sum(probs * grad_probs, axis=-1, keepdims=True)
                )
                half = grad_scores.astype(jnp.bfloat16)
                grad_query = (mm(half, k, NN) * scale).astype(jnp.bfloat16)
                grad_key = (mm(half, q, TN) * scale).astype(jnp.bfloat16)
                stacked.append((grad_query, grad_key, grad_value))
                if t == 0:
                    total[step * pair + h] = grad_scores
                else:
                    total[step * pair + h] += grad_scores
            back = [
                mm(jnp.concatenate(g, axis=1), in_block(step, c), NT)
                for c, g in enumerate(zip(*stacked))
            ]
            acc[...] += back[0] + back[1] + back[2]
            return carry

        lax.fori_loop(0, steps, run, 0)

    def tables(low, high):
        def run(b, carry):
            chosen = buckets[...] == b
            sums[b] = jnp.concatenate(
                [
                    jnp.sum(jnp.where(chosen, total[h], 0.0), axis=0, keepdims=True)
                    for h in range(total.shape[0])
                ],
                axis=0,
            )
            return carry

        lax.fori_loop(low, high, run, 0)

    for step in range(steps):
        for c in range(3):
            load(step, c).start()
    barrier = pltpu.get_barrier_semaphore()
    greeted = [twin] + [peer(k) * 2 + core for k in range(1, chips)]
    for other in greeted:
        pl.semaphore_signal(barrier, inc=1, device_id={"head": other}, device_id_type=MESH)

    @pl.when(section > 0)
    def _():
        pl.semaphore_signal(
            barrier, inc=1, device_id={"section": section - 1}, device_id_type=MESH
        )

    @pl.when(section < sections - 1)
    def _():
        pl.semaphore_signal(
            barrier, inc=1, device_id={"section": section + 1}, device_id_type=MESH
        )

    cur[0, 0] = rising[...]
    cur[1, 0] = falling[...]
    flat_down[...] = flat(falling[...]).astype(jnp.bfloat16)
    normalize(0, flat(rising[...]))
    for t in range(ticks):
        normalize(t + 1, flat(stash[t]))
    pl.semaphore_wait(
        barrier,
        len(greeted)
        + (section > 0).astype(jnp.int32)
        + (section < sections - 1).astype(jnp.int32),
    )
    for t in range(ticks):
        if t > 0:
            settle(0, t - 1)
            normalize(0, flat(cur[0, t]))
        acc[...] = jnp.zeros_like(acc)
        forward(t)
        begin(0, t)
        if t > 0:
            settle(1, t - 1)
            flat_down[...] = flat(cur[1, t]).astype(jnp.bfloat16)
        acc[...] = jnp.zeros_like(acc)
        backward(t)
        begin(1, t)
    last = ticks - 1
    settle(0, last)
    moved[0] = cur[0, ticks]
    count = sums.shape[0]
    for i, (stage, _at) in enumerate(stages):
        tables(i * count // 3, (i + 1) * count // 3)
        stage(1, last)
    table[...] = jnp.sum(sums[...], axis=-1)
    settle(1, last)
    moved[1] = cur[1, ticks]


def per_device(rising, falling, stash, queue, order, buckets, bias_table, gain, w_qkv, w_out):
    sections = lax.axis_size("section")
    head_count = lax.axis_size("head")
    ticks = stash.shape[1]
    rows, width = rising.shape[1:]
    heads, head_dim = w_qkv.shape[2], w_qkv.shape[4]
    chips, part_rows = head_count // 2, rows // head_count
    pair = next(p for p in (4, 4, 2, 1) if heads % p == 0)
    steps, span = heads // pair, pair * head_dim
    others = max(chips - 1, 1)
    w_in = jnp.swapaxes(w_qkv[0], 1, 2).reshape(width, 3 * heads * head_dim)
    w_back = w_out[0].reshape(heads * head_dim, width)
    bucket_ids = jnp.arange(bias_table.shape[1], dtype=jnp.int32)
    onehot = (buckets[None, :, :] == bucket_ids[:, None, None]).astype(jnp.float32)
    biases = jnp.einsum("bij,bh->hij", onehot, bias_table[0], precision=lax.Precision.HIGHEST)
    split = lambda a: a.reshape(a.shape[:-2] + (chips, 2, part_rows, width))
    vmem = pl.BlockSpec(memory_space=pltpu.VMEM)
    tile = (part_rows, width)
    bf16 = lambda *shape: pltpu.VMEM(shape, jnp.bfloat16)
    dma = lambda *shape: pltpu.SemaphoreType.DMA(shape)
    moved, table = pl.pallas_call(
        functools.partial(wave_kernel, ticks, steps, pair, head_dim, chips, sections),
        in_specs=[pl.BlockSpec(memory_space=pltpu.SMEM)] + [vmem] * 7 + [pl.BlockSpec(memory_space=pl.ANY), vmem],
        out_specs=[vmem] * 2,
        out_shape=[
            jax.ShapeDtypeStruct((2, chips, 2) + tile, jnp.bfloat16),
            jax.ShapeDtypeStruct((bias_table.shape[1], heads), jnp.float32),
        ],
        scratch_shapes=[
            bf16(steps, 3, width, span),
            dma(steps, 3),
            bf16((ticks + 1) * rows, width),
            bf16(steps, 3, ticks * rows, span),
            bf16(rows, width),
            pltpu.VMEM((rows, width), jnp.float32),
            pltpu.VMEM((heads, rows, rows), jnp.float32),
            pltpu.VMEM((bias_table.shape[1], heads, rows), jnp.float32),
            bf16(2, ticks + 1, chips, 2, *tile),
            bf16(2, ticks, chips, 2, *tile),
            bf16(2, ticks, chips, *tile),
            bf16(2, ticks, others, *tile),
            bf16(2, ticks, others, *tile),
            bf16(2, ticks, *tile),
            dma(2, ticks, chips), dma(2, ticks, chips),
            dma(2, ticks, others), dma(2, ticks, others),
            dma(2, ticks), dma(2, ticks),
            dma(2, ticks, others), dma(2, ticks, others),
            dma(2, ticks, chips), dma(2, ticks, chips),
        ],
        compiler_params=pltpu.CompilerParams(
            collective_id=0, has_side_effects=True, vmem_limit_bytes=40 << 20
        ),
    )(
        order, split(rising[0]), split(falling[0]), split(stash[0]), split(queue), gain,
        biases, buckets, w_in, w_back,
    )
    moved = moved.reshape(2, 1, rows, width)
    return (moved[0], moved[1], table[None])


def solution(mesh):
    return jax.shard_map(
        per_device,
        mesh=mesh,
        in_specs=(
            P(("groups", "section"), None, None),
            P(("groups", "section"), None, None),
            P(("groups", "section"), None, None, None),
            P("groups", None, None),
            P("groups"),
            P(),
            P("section", None, "head"),
            P("section", None),
            P("section", None, "head", None, None),
            P("section", "head", None, None),
        ),
        out_specs=(
            P(("groups", "section"), None, None),
            P(("groups", "section"), None, None),
            P(("groups", "section"), None, "head"),
        ),
        check_vma=False,
    )
```

profile of v0, /device:TPU:0, one launch (start us, length us, event | category | flops | bytes accessed | tf_op | source)
XLA Modules:
  0.0 115.3 jit_solution(2983665819503673934)
XLA Ops:
  0.6 0.0 copy-start
  0.6 0.7 copy-done
  1.3 1.6 %fusion = f32[128,128,16]{1,2,0:T(8,128)S(1)} fusion(s32[128,128]{1,0:T(8,128)} %buckets.1, f32[1,32,16]{1,2,0:T(8,128)S(1)} %copy-done), kind=kOutput, calls=%fused_computation.2 | convolution fusion | flops 101187584 | bytes 1116160 | tf_op jit(solution)/shard_map/bij,bh->hij/dot_general | solution.py:353
  2.9 0.3 copy.19
  3.3 0.0 copy-start.1
  3.3 0.0 copy-start.2
  3.3 0.0 copy-start.3
  3.3 0.0 copy-start.4
  3.3 0.0 copy-start.5
  3.3 0.0 copy-start.6
  3.3 0.0 copy-start.7
  3.4 0.0 copy-start.8
  3.4 14.0 %copy.18 = bf16[128,8,48,128]{3,1,2,0:T(8,128)(2,1)} copy(bf16[128,8,48,128]{3,2,1,0:T(8,128)(2,1)} %bitcast.31) | data formatting | bytes 25165824
  17.4 0.0 copy-done.1
  17.4 0.0 copy-done.2
  17.4 0.0 copy-done.3
  17.4 0.0 copy-done.4
  17.4 0.0 copy-done.5
  17.4 0.0 copy-done.6
  17.4 0.0 copy-done.7
  17.4 0.0 copy-done.8
  17.4 96.4 %shard_map.121 = (bf16[2,2,2,32,1024]{4,3,2,1,0:T(8,128)(2,1)S(1)}, f32[32,16]{1,0:T(8,128)S(1)}) custom-call(s32[6]{0:T(128)S(1)} %copy-done.8, bf16[2,2,32,1024]{3,2,1,0:T(8,128)(2,1)S(1)} %bitcast.27, bf16[2,2,32,1024]{3,2,1,0:T(8,128)(2,1)S(1)} %bitcast.28, bf16[3,2,2,32,1024]{4,3,2,1,0:T(8,128)(2,1)S(1)} %bitcast.26, ...), custom_call_target="tpu_custom_call" | custom-call | tf_op jit(solution)/shard_map/pallas_call | solution.py:359
  113.8 0.7 copy.14
  114.5 0.8 fusion.3
Async XLA Ops:
  0.6 0.7 copy-start
  3.3 14.1 %copy-start.1 = (bf16[1,16,128,1024]{3,2,1,0:T(8,128)(2,1)S(1)}, bf16[1,16,128,1024]{3,2,1,0:T(8,128)(2,1)}, u32[]{:S(2)}) copy-start(bf16[1,16,128,1024]{3,2,1,0:T(8,128)(2,1)} %param.19) | copy-start | bytes 12582916
  3.3 14.1 %copy-start.2 = (bf16[6,128,1024]{2,1,0:T(8,128)(2,1)S(1)}, bf16[6,128,1024]{2,1,0:T(8,128)(2,1)}, u32[]{:S(2)}) copy-start(bf16[6,128,1024]{2,1,0:T(8,128)(2,1)} %param.13) | copy-start | bytes 4718596
  3.3 14.1 %copy-start.3 = (bf16[1,3,128,1024]{3,2,1,0:T(8,128)(2,1)S(1)}, bf16[1,3,128,1024]{3,2,1,0:T(8,128)(2,1)}, u32[]{:S(2)}) copy-start(bf16[1,3,128,1024]{3,2,1,0:T(8,128)(2,1)} %param.12) | copy-start | bytes 2359300
  3.3 14.1 %copy-start.4 = (bf16[1,128,1024]{2,1,0:T(8,128)(2,1)S(1)}, bf16[1,128,1024]{2,1,0:T(8,128)(2,1)}, u32[]{:S(2)}) copy-start(bf16[1,128,1024]{2,1,0:T(8,128)(2,1)} %param.10) | copy-start | bytes 786436
  3.3 14.1 %copy-start.5 = (bf16[1,128,1024]{2,1,0:T(8,128)(2,1)S(1)}, bf16[1,128,1024]{2,1,0:T(8,128)(2,1)}, u32[]{:S(2)}) copy-start(bf16[1,128,1024]{2,1,0:T(8,128)(2,1)} %param.11) | copy-start | bytes 786436
  3.3 14.1 %copy-start.6 = (s32[128,128]{1,0:T(8,128)S(1)}, s32[128,128]{1,0:T(8,128)}, u32[]{:S(2)}) copy-start(s32[128,128]{1,0:T(8,128)} %buckets.1) | copy-start | bytes 196612
  3.3 14.1 %copy-start.7 = (f32[1,1024]{1,0:T(1,128)S(1)}, f32[1,1024]{1,0:T(1,128)}, u32[]{:S(2)}) copy-start(f32[1,1024]{1,0:T(1,128)} %gain.1) | copy-start | bytes 12292
  3.4 14.1 %copy-start.8 = (s32[6]{0:T(128)S(1)}, s32[6]{0:T(128)}, u32[]{:S(2)}) copy-start(s32[6]{0:T(128)} %order.1) | copy-start | bytes 76
where the time goes:
time: 116 us; the launch traced here: 115 us
  Pallas kernels  96.4 us (83%)
  local copies, waits for them, and re-layouts  16.6 us (14%)
  matrix products  1.59 us (1%)
    pallas_call x1, Pallas kernels, per_device(): pl.pallas_call(functools.partial(wave_kernel, ticks, steps, pair, head_di...  96.4 us
    unnamed x20, local copies, waits for them, and re-layouts  15.4 us

commit v1 on v0

v1 whole, which is shorter than its diff:
```python
import functools

import jax
import jax.numpy as jnp
from jax import lax
from jax.experimental import pallas as pl
from jax.experimental.pallas import tpu as pltpu
from jax.sharding import PartitionSpec as P

EPSILON = 1e-06
MESH = pl.DeviceIdType.MESH
NN = (((1,), (0,)), ((), ()))
NT = (((1,), (1,)), ((), ()))
TN = (((0,), (0,)), ((), ()))
BF16 = jnp.bfloat16
F32 = jnp.float32


def mm(a, b, dims):
    return lax.dot_general(a, b, dims, preferred_element_type=F32)


def inverse_rms(x):
    return lax.rsqrt(jnp.mean(x * x, axis=-1, keepdims=True) + EPSILON)


def softmax(scores):
    raised = jnp.exp(scores - jnp.max(scores, axis=-1, keepdims=True))
    return raised * (1.0 / jnp.sum(raised, axis=-1, keepdims=True))


def wave_kernel(
    ticks, pair, head_dim, chips, sections, halves, group,
    order, rising, falling, stash, queue, gain, labels, buckets, w_hbm, wo_hbm,
    moved, table,
    bias, raw, w_sem, wo, wo_sem, wq, wk, wv, aq, ak, av, normed, probs, attended,
    gflat, gq, gk, gv, thin, flat_down, total, sums,
    cur, part, near, away, far, share,
    near_send, near_recv, far_send, far_recv,
    lift_send, lift_recv, gather_send, gather_recv, pass_send, pass_recv,
):
    section = lax.axis_index("section")
    head = lax.axis_index("head")
    chip, core = head // 2, lax.rem(head, 2)
    twin = chip * 2 + (1 - core)
    heads, rows = total.shape[:2]
    lanes = flat_down.shape[2]
    tiles = flat_down.shape[0]
    width = tiles * lanes
    steps = heads // pair
    scale = head_dim ** (-0.5)
    half = width // halves
    weights, acts, grads = (wq, wk, wv), (aq, ak, av), (gq, gk, gv)
    last = ticks - 1

    def peer(k):
        return lax.rem(chip + k, chips)

    def remote(src, dst, send, recv, target):
        return pltpu.make_async_remote_copy(
            src_ref=src, dst_ref=dst, send_sem=send, recv_sem=recv,
            device_id=target, device_id_type=MESH,
        )

    def flat(x):
        return x.astype(F32).reshape(rows, width)

    def cut(j):
        return pl.ds(j * half, half)

    def near_copy(which, t, j, k):
        return remote(
            part.at[which, t, peer(k), 1 - core, :, cut(j)], near.at[which, t, k, :, cut(j)],
            near_send.at[which, t, j, k], near_recv.at[which, t, j, k], {"head": twin},
        )

    def far_copy(which, t, j, k):
        return remote(
            away.at[which, t, k - 1, :, cut(j)], far.at[which, t, k - 1, :, cut(j)],
            far_send.at[which, t, j, k - 1], far_recv.at[which, t, j, k - 1],
            {"head": peer(k) * 2 + core},
        )

    def lift_copy(which, t, j, target):
        return remote(
            share.at[which, t, :, cut(j)], cur.at[which, t + 1, chip, core, :, cut(j)],
            lift_send.at[which, t, j], lift_recv.at[which, t, j], {"section": target},
        )

    def gather_copy(which, t, j, k):
        rows_here = cur.at[which, t + 1, chip, core, :, cut(j)]
        return remote(
            rows_here, rows_here,
            gather_send.at[which, t, j, k - 1], gather_recv.at[which, t, j, k - 1],
            {"head": peer(k) * 2 + core},
        )

    def pass_copy(which, t, j, k):
        rows_here = cur.at[which, t + 1, lax.rem(chip - k + chips, chips), core, :, cut(j)]
        return remote(
            rows_here, rows_here,
            pass_send.at[which, t, j, k], pass_recv.at[which, t, j, k], {"head": twin},
        )

    def begin(which, t, j):
        for k in list(range(1, chips)) + [0]:
            near_copy(which, t, j, k).start()

    def fold(which, t, j):
        for k in range(1, chips):
            near_copy(which, t, j, k).wait_recv()
            away[which, t, k - 1, :, cut(j)] = (
                part[which, t, peer(k), core, :, cut(j)].astype(F32)
                + near[which, t, k, :, cut(j)].astype(F32)
            ).astype(BF16)
            far_copy(which, t, j, k).start()

    def ends(which):
        if which == 0:
            return section < sections - 1, section + 1, section > 0, section - 1
        return section > 0, section - 1, section < sections - 1, section + 1

    def reduced(which, t, j):
        near_copy(which, t, j, 0).wait_recv()
        own = part[which, t, chip, core, :, cut(j)].astype(F32) + near[
            which, t, 0, :, cut(j)
        ].astype(F32)
        for k in range(1, chips):
            far_copy(which, t, j, k).wait_recv()
            own = own + far[which, t, k - 1, :, cut(j)].astype(F32)
        return own

    def hand_on(which, t, j, result):
        sends, target, receives, _ = ends(which)
        if t == last:
            cur[which, t + 1, chip, core, :, cut(j)] = result
            return
        share[which, t, :, cut(j)] = result

        @pl.when(sends)
        def _():
            lift_copy(which, t, j, target).start()

        @pl.when(jnp.logical_not(receives))
        def _():
            if which == 0:
                cur[which, t + 1, chip, core, :, cut(j)] = queue[
                    order[t], chip, core, :, cut(j)
                ]
            else:
                cur[which, t + 1, chip, core, :, cut(j)] = share[0, t, :, cut(j)]

    def finish_up(t, j):
        before = cur[0, t, chip, core, :, cut(j)].astype(F32)
        hand_on(0, t, j, (before + reduced(0, t, j)).astype(BF16))

    def finish_down(t):
        own = jnp.concatenate([reduced(1, t, j) for j in range(halves)], axis=-1)
        before = cur[1, t, chip, core].astype(F32)
        x = stash[t, chip, core].astype(F32)
        inverse = inverse_rms(x)
        cubed = inverse * inverse * inverse
        weighted = gain[...] * own
        result = (
            before
            + inverse * weighted
            - x * cubed * jnp.mean(x * weighted, axis=-1, keepdims=True)
        ).astype(BF16)
        for j in range(halves):
            hand_on(1, t, j, result[:, j * half : (j + 1) * half])

    def spread(which, t, j):
        _, _, receives, source = ends(which)
        if t < last:
            @pl.when(receives)
            def _():
                lift_copy(which, t, j, source).wait_recv()

        for k in range(1, chips):
            gather_copy(which, t, j, k).start()
        pass_copy(which, t, j, 0).start()

    def relay(which, t, j):
        for k in range(1, chips):
            gather_copy(which, t, j, k).wait_recv()
            pass_copy(which, t, j, k).start()

    def settle(which, t):
        sends, target, _, _ = ends(which)
        for j in range(halves):
            for k in range(chips):
                pass_copy(which, t, j, k).wait_recv()
        for j in range(halves):
            for k in range(chips):
                near_copy(which, t, j, k).wait_send()
                pass_copy(which, t, j, k).wait_send()
            for k in range(1, chips):
                far_copy(which, t, j, k).wait_send()
                gather_copy(which, t, j, k).wait_send()
            if t < last:
                @pl.when(sends)
                def _(j=j):
                    lift_copy(which, t, j, target).wait_send()

    def beside(blocks):
        return jnp.concatenate(blocks, axis=1)

    def fetch(c):
        return pltpu.make_async_copy(w_hbm.at[:, c], raw.at[c % 2], w_sem.at[c])

    def relay_weights(c, low, count):
        for n in range(count):
            at = pl.ds(pl.multiple_of((low + n) * group, group), group)
            turned = jnp.swapaxes(raw[c % 2, at], 0, 1)
            for h in range(heads):
                weights[c][h, at] = turned[h]

    def normalize(place, x):
        y = (x * inverse_rms(x) * gain[...]).astype(BF16)
        for b in range(tiles):
            normed[b, place * rows : (place + 1) * rows] = y[:, b * lanes : (b + 1) * lanes]

    def lower(x):
        y = x.astype(BF16)
        for b in range(tiles):
            flat_down[b] = y[:, b * lanes : (b + 1) * lanes]

    def project(c, step, place, count=1):
        at = slice(place * rows, (place + count) * rows)
        result = mm(
            beside([normed[b, at] for b in range(tiles)]),
            beside([weights[c][step * pair + h] for h in range(pair)]),
            NN,
        ).astype(BF16)
        for h in range(pair):
            acts[c][step * pair + h, at] = result[:, h * head_dim : (h + 1) * head_dim]

    def project_pairs(place):
        def run(step, carry):
            project(0, step, place)
            project(1, step, place)
            return carry

        lax.fori_loop(0, steps, run, 0)

    def block(emit):
        pl.when(section >= 0)(emit)

    def act(c, place, n):
        return acts[c][n, place * rows : (place + 1) * rows]

    def score(place, step):
        return [
            mm(act(0, place, n), act(1, place, n), NT) * scale + bias[n]
            for n in range(step * pair, (step + 1) * pair)
        ]

    def hooked(hooks, n):
        for action in hooks.get(n, ()):
            action()

    def blend(t, step, scores):
        for h in range(pair):
            probs16 = softmax(scores[h]).astype(BF16)
            n = step * pair + h
            attended[n] = mm(probs16, act(2, 0, n), NN).astype(BF16)

    def keep(step, scores):
        for h in range(pair):
            probs[step * pair + h] = softmax(scores[h])

    def out(t, hooks, base):
        for j in range(halves):
            each = half // lanes
            right = beside([wo[b] for b in range(j * each, (j + 1) * each)])
            left = beside([attended[n] for n in range(heads)])
            result = mm(left, right, NN).astype(BF16)
            part[0, t, :, :, :, cut(j)] = result.reshape(part.shape[2:5] + (half,))
            begin(0, t, j)
            hooked(hooks, base + j)

    def forward(t, hooks, also=None):
        count = 1 if also is None else 2
        if also is None:
            project_pairs(0)
            hooked(hooks, 0)

        @functools.partial(block)
        def _():
            scores = {n: score(0, n) for n in range(min(2, steps))}
            for step in range(steps):
                project(2, step, 0, count)
                extra = score(also, step) if also is not None else None
                if 2 <= step + 2 < steps:
                    scores[step + 2] = score(0, step + 2)
                blend(t, step, scores.pop(step))
                if extra is not None:
                    keep(step, extra)
                hooked(hooks, 2 + step)
            out(t, hooks, 2 + steps)

    def fill(place, hooks):
        project_pairs(place)
        hooked(hooks, 0)

        @functools.partial(block)
        def _():
            scores = {n: score(place, n) for n in range(min(2, steps))}
            for step in range(steps):
                project(2, step, place)
                if step + 2 < steps:
                    scores[step + 2] = score(place, step + 2)
                keep(step, scores.pop(step))
        hooked(hooks, 1 + steps)

    def backward(t, hooks):
        place = t + 1

        def open_grad(step):
            block = slice(step * pair * head_dim, (step + 1) * pair * head_dim)
            result = mm(
                beside([flat_down[b] for b in range(tiles)]),
                beside([wo[b, block] for b in range(tiles)]),
                NT,
            ).astype(BF16)
            for h in range(pair):
                gflat[step * pair + h] = result[:, h * head_dim : (h + 1) * head_dim]

        def score_grads(step):
            for h in range(pair):
                n = step * pair + h
                g = gflat[n]
                grad_probs = mm(g, act(2, place, n), NT)
                p = probs[n]
                gv[n] = mm(p.astype(BF16), g, TN).astype(BF16)
                grad_scores = p * (
                    grad_probs - jnp.sum(p * grad_probs, axis=-1, keepdims=True)
                )
                thin[step % 2, h] = grad_scores.astype(BF16)
                if t == 0:
                    total[n] = grad_scores
                else:
                    total[n] += grad_scores

        def query_key_grads(step):
            for h in range(pair):
                n = step * pair + h
                small = thin[step % 2, h]
                gq[n] = (mm(small, act(1, place, n), NN) * scale).astype(BF16)
                gk[n] = (mm(small, act(0, place, n), TN) * scale).astype(BF16)

        @functools.partial(block)
        def _():
            open_grad(0)
            for step in range(steps):
                score_grads(step)
                if step + 1 < steps:
                    open_grad(step + 1)
                if step > 0:
                    query_key_grads(step - 1)
                hooked(hooks, step)
            query_key_grads(steps - 1)

        for j in range(halves):
            @functools.partial(block)
            def _(j=j):
                rows_of = slice(j * half, (j + 1) * half)
                back = [
                    mm(
                        beside([grads[c][n] for n in range(heads)]),
                        beside([weights[c][n, rows_of] for n in range(heads)]),
                        NT,
                    )
                    for c in (2, 0, 1)
                ]
                result = (back[0] + back[1] + back[2]).astype(BF16)
                part[1, t, :, :, :, cut(j)] = result.reshape(part.shape[2:5] + (half,))
                begin(1, t, j)
                hooked(hooks, steps + j)

    def tables(low, high):
        def run(b, carry):
            chosen = buckets[...] == b
            sums[b] = jnp.concatenate(
                [
                    jnp.sum(jnp.where(chosen, total[h], 0.0), axis=0, keepdims=True)
                    for h in range(total.shape[0])
                ],
                axis=0,
            )
            return carry

        lax.fori_loop(low, high, run, 0)

    def fetch_out(b):
        return pltpu.make_async_copy(
            wo_hbm.at[:, pl.ds(b * lanes, lanes)], wo.at[b], wo_sem.at[b]
        )

    fetch(0).start()
    fetch(1).start()
    barrier = pltpu.get_barrier_semaphore()
    greeted = [twin] + [peer(k) * 2 + core for k in range(1, chips)]
    for other in greeted:
        pl.semaphore_signal(barrier, inc=1, device_id={"head": other}, device_id_type=MESH)

    @pl.when(section > 0)
    def _():
        pl.semaphore_signal(
            barrier, inc=1, device_id={"section": section - 1}, device_id_type=MESH
        )

    @pl.when(section < sections - 1)
    def _():
        pl.semaphore_signal(
            barrier, inc=1, device_id={"section": section + 1}, device_id_type=MESH
        )

    blank = jnp.zeros((heads, lanes - labels.shape[1]), F32)
    lookup = jnp.concatenate([labels[...], blank], axis=1)
    for n in range(heads):
        bias[n] = jnp.take_along_axis(
            jnp.broadcast_to(lookup[n : n + 1], (rows, lanes)), buckets[...], axis=1
        )
    cur[0, 0] = rising[...]
    cur[1, 0] = falling[...]
    lower(flat(falling[...]))
    normalize(0, flat(rising[...]))
    for t in range(ticks):
        normalize(t + 1, flat(stash[t]))

    blocks = width // group
    fetch(0).wait()

    def first(n, carry):
        relay_weights(0, n * 4, 4)
        return carry

    lax.fori_loop(0, blocks // 4, first, 0)
    fetch(2).start()
    for b in range(tiles):
        fetch_out(b).start()

    for c in (1, 2):
        fetch(c).wait()

        def under(step, carry, c=c):
            project(c - 1, step, 0, 2)
            relay_weights(c, step * (blocks // steps), blocks // steps)
            return carry

        lax.fori_loop(0, steps, under, 0)
    for b in range(tiles):
        fetch_out(b).wait()
    pl.semaphore_wait(
        barrier,
        len(greeted)
        + (section > 0).astype(jnp.int32)
        + (section < sections - 1).astype(jnp.int32),
    )

    def do(function, *args):
        return lambda: function(*args)

    def both(function, which, t):
        return [do(function, which, t, j) for j in range(halves)]

    s = steps
    forward(0, {}, also=1)
    for t in range(ticks):
        backward(t, {
            0: both(fold, 0, t),
            s - 1 if s > 1 else 1: [do(finish_up, t, 0)],
            s: [do(finish_up, t, j) for j in range(1, halves)],
            s + halves - 1: both(spread, 0, t),
        })
        if t < last:
            fill(t + 2, {
                0: both(fold, 1, t),
                1 + s: [do(finish_down, t)] + both(relay, 0, t),
            })
            settle(0, t)
            normalize(0, flat(cur[0, t + 1]))
            forward(t + 1, {
                2: both(spread, 1, t),
                1 + s + halves: both(relay, 1, t),
            })
            settle(1, t)
            lower(flat(cur[1, t + 1]))
    count = sums.shape[0]
    tables(0, count // 5)
    for action in both(fold, 1, last) + both(relay, 0, last):
        action()
    settle(0, last)
    moved[0] = cur[0, ticks]
    tables(count // 5, count * 7 // 10)
    finish_down(last)
    for action in both(spread, 1, last):
        action()
    tables(count * 7 // 10, count)
    table[...] = jnp.sum(sums[...], axis=-1)
    for action in both(relay, 1, last):
        action()
    settle(1, last)
    moved[1] = cur[1, ticks]


def per_device(rising, falling, stash, queue, order, buckets, bias_table, gain, w_qkv, w_out):
    sections = lax.axis_size("section")
    head_count = lax.axis_size("head")
    ticks = stash.shape[1]
    rows, width = rising.shape[1:]
    heads, head_dim = w_qkv.shape[2], w_qkv.shape[4]
    chips, part_rows = head_count // 2, rows // head_count
    pair = next(p for p in (4, 2, 1) if heads % p == 0)
    others = max(chips - 1, 1)
    halves, group, lanes = 2, 16, 128
    flat_heads = heads * head_dim
    w_in = jnp.swapaxes(w_qkv[0], 1, 2)
    w_back = w_out[0].reshape(flat_heads, width)
    split = lambda a: a.reshape(a.shape[:-2] + (chips, 2, part_rows, width))
    vmem = pl.BlockSpec(memory_space=pltpu.VMEM)
    tile = (part_rows, width)
    bf16 = lambda *shape: pltpu.VMEM(shape, BF16)
    f32 = lambda *shape: pltpu.VMEM(shape, F32)
    dma = lambda *shape: pltpu.SemaphoreType.DMA(shape)
    moved, table = pl.pallas_call(
        functools.partial(
            wave_kernel, ticks, pair, head_dim, chips, sections, halves, group
        ),
        in_specs=[pl.BlockSpec(memory_space=pltpu.SMEM)] + [vmem] * 7 + [pl.BlockSpec(memory_space=pl.ANY)] * 2,
        out_specs=[vmem] * 2,
        out_shape=[
            jax.ShapeDtypeStruct((2, chips, 2) + tile, BF16),
            jax.ShapeDtypeStruct((bias_table.shape[1], heads), F32),
        ],
        scratch_shapes=[
            f32(heads, rows, rows),
            bf16(2, width, heads, head_dim),
            dma(3),
            bf16(width // lanes, flat_heads, lanes),
            dma(width // lanes),
            bf16(heads, width, head_dim),
            bf16(heads, width, head_dim),
            bf16(heads, width, head_dim),
            bf16(heads, (ticks + 1) * rows, head_dim),
            bf16(heads, (ticks + 1) * rows, head_dim),
            bf16(heads, (ticks + 1) * rows, head_dim),
            bf16(width // lanes, (ticks + 1) * rows, lanes),
            f32(heads, rows, rows),
            bf16(heads, rows, head_dim),
            bf16(heads, rows, head_dim),
            bf16(heads, rows, head_dim),
            bf16(heads, rows, head_dim),
            bf16(heads, rows, head_dim),
            bf16(2, pair, rows, rows),
            bf16(width // lanes, rows, lanes),
            f32(heads, rows, rows),
            f32(bias_table.shape[1], heads, rows),
            bf16(2, ticks + 1, chips, 2, *tile),
            bf16(2, ticks, chips, 2, *tile),
            bf16(2, ticks, chips, *tile),
            bf16(2, ticks, others, *tile),
            bf16(2, ticks, others, *tile),
            bf16(2, ticks, *tile),
            dma(2, ticks, halves, chips), dma(2, ticks, halves, chips),
            dma(2, ticks, halves, others), dma(2, ticks, halves, others),
            dma(2, ticks, halves), dma(2, ticks, halves),
            dma(2, ticks, halves, others), dma(2, ticks, halves, others),
            dma(2, ticks, halves, chips), dma(2, ticks, halves, chips),
        ],
        compiler_params=pltpu.CompilerParams(
            collective_id=0, has_side_effects=True, vmem_limit_bytes=52 << 20
        ),
    )(
        order, split(rising[0]), split(falling[0]), split(stash[0]), split(queue), gain,
        bias_table[0].T, buckets, w_in, w_back,
    )
    moved = moved.reshape(2, 1, rows, width)
    return (moved[0], moved[1], table[None])


def solution(mesh):
    return jax.shard_map(
        per_device,
        mesh=mesh,
        in_specs=(
            P(("groups", "section"), None, None),
            P(("groups", "section"), None, None),
            P(("groups", "section"), None, None, None),
            P("groups", None, None),
            P("groups"),
            P(),
            P("section", None, "head"),
            P("section", None),
            P("section", None, "head", None, None),
            P("section", "head", None, None),
        ),
        out_specs=(
            P(("groups", "section"), None, None),
            P(("groups", "section"), None, None),
            P(("groups", "section"), None, "head"),
        ),
        check_vma=False,
    )
```

time: 116 us -> 88.6 us (0.76)
  Pallas kernels: 96.4 us -> 80.2 us
  local copies, waits for them, and re-layouts: 16.6 us -> 7.41 us
  matrix products: 1.59 us -> 0 us
    pallas_call x1, Pallas kernels: 96.4 us -> 80.2 us  [per_device(): pl.pallas_call(functools.partial(wave_kernel, ticks, pair, head_dim, chip...]
    unnamed x20 -> x15, local copies, waits for them, and re-layouts: 15.4 us -> 6.57 us
    dot_general x1 -> x0, matrix products: 1.59 us -> none  [per_device(): jnp.einsum('bij,bh->hij', onehot, bias_table[0], precision=lax.Precision....]
where the time goes in v1:
time: 88.6 us; the launch traced here: 88.3 us
  Pallas kernels  80.2 us (91%)
  local copies, waits for them, and re-layouts  7.41 us (8%)
    pallas_call x1, Pallas kernels, per_device(): pl.pallas_call(functools.partial(wave_kernel, ticks, pair, head_dim, chip...  80.2 us
    unnamed x15, local copies, waits for them, and re-layouts  6.57 us

profile of v1, /device:TPU:0, one launch (start us, length us, event | category | flops | bytes accessed | tf_op | source)
XLA Modules:
  0.0 88.3 jit_solution(421429631566942866)
XLA Ops:
  0.6 0.0 copy-start
  0.6 1.1 %copy-done = bf16[1,3,128,1024]{3,2,1,0:T(8,128)(2,1)S(1)} copy-done((bf16[1,3,128,1024]{3,2,1,0:T(8,128)(2,1)S(1)}, bf16[1,3,128,1024]{3,2,1,0:T(8,128)(2,1)}, u32[]{:S(2)}) %copy-start) | copy-done | bytes 786456
  1.8 0.0 copy-start.1
  1.8 0.9 %copy-done.1 = bf16[1,128,1024]{2,1,0:T(8,128)(2,1)S(1)} copy-done((bf16[1,128,1024]{2,1,0:T(8,128)(2,1)S(1)}, bf16[1,128,1024]{2,1,0:T(8,128)(2,1)}, u32[]{:S(2)}) %copy-start.1) | copy-done | bytes 262168
  2.7 0.0 copy-start.2
  2.7 0.9 %copy-done.2 = bf16[1,128,1024]{2,1,0:T(8,128)(2,1)S(1)} copy-done((bf16[1,128,1024]{2,1,0:T(8,128)(2,1)S(1)}, bf16[1,128,1024]{2,1,0:T(8,128)(2,1)}, u32[]{:S(2)}) %copy-start.2) | copy-done | bytes 262168
  3.7 0.0 copy-start.3
  3.7 0.8 copy-done.3
  4.5 0.0 copy-start.4
  4.5 0.7 copy-done.4
  5.2 0.0 copy-start.5
  5.2 0.7 copy-done.5
  5.9 0.0 copy-start.6
  5.9 0.7 copy-done.6
  6.5 80.2 %shard_map.121 = (bf16[2,2,2,32,1024]{4,3,2,1,0:T(8,128)(2,1)S(1)}, f32[32,16]{1,0:T(8,128)S(1)}) custom-call(s32[6]{0:T(128)S(1)} %copy-done.6, bf16[2,2,32,1024]{3,2,1,0:T(8,128)(2,1)S(1)} %bitcast.15, bf16[2,2,32,1024]{3,2,1,0:T(8,128)(2,1)S(1)} %bitcast.16, bf16[3,2,2,32,1024]{4,3,2,1,0:T(8,128)(2,1)S(1)} %bitcast.14, ...), custom_call_target="tpu_custom_call" | custom-call | tf_op jit(solution)/shard_map/pallas_call | solution.py:527
  86.7 0.7 copy.13
  87.4 0.8 fusion
Async XLA Ops:
  0.6 1.1 %copy-start = (bf16[1,3,128,1024]{3,2,1,0:T(8,128)(2,1)S(1)}, bf16[1,3,128,1024]{3,2,1,0:T(8,128)(2,1)}, u32[]{:S(2)}) copy-start(bf16[1,3,128,1024]{3,2,1,0:T(8,128)(2,1)} %param.12) | copy-start | bytes 2359300
  1.8 0.9 %copy-start.1 = (bf16[1,128,1024]{2,1,0:T(8,128)(2,1)S(1)}, bf16[1,128,1024]{2,1,0:T(8,128)(2,1)}, u32[]{:S(2)}) copy-start(bf16[1,128,1024]{2,1,0:T(8,128)(2,1)} %param.10) | copy-start | bytes 786436
  2.7 0.9 %copy-start.2 = (bf16[1,128,1024]{2,1,0:T(8,128)(2,1)S(1)}, bf16[1,128,1024]{2,1,0:T(8,128)(2,1)}, u32[]{:S(2)}) copy-start(bf16[1,128,1024]{2,1,0:T(8,128)(2,1)} %param.11) | copy-start | bytes 786436
  3.7 0.8 copy-start.3
  4.5 0.7 copy-start.4
  5.2 0.7 copy-start.5
  5.9 0.7 copy-start.6

commit v2 on v1

--- a/solution.py
+++ b/solution.py
@@ -30,13 +30,15 @@
 
 
 def wave_kernel(
-    ticks, pair, head_dim, chips, sections, halves, group,
-    order, rising, falling, stash, queue, gain, labels, buckets, w_hbm, wo_hbm,
+    ticks, pair, head_dim, chips, sections, halves, pieces, group,
+    order, rising, falling, stash_hbm, queue_hbm, gain_hbm, labels_hbm, buckets_hbm,
+    w_hbm, wo_hbm,
     moved, table,
+    stash, queue, gain, labels, buckets, in_sem,
     bias, raw, w_sem, wo, wo_sem, wq, wk, wv, aq, ak, av, normed, probs, attended,
     gflat, gq, gk, gv, thin, flat_down, total, sums,
-    cur, part, near, away, far, share,
-    near_send, near_recv, far_send, far_recv,
+    cur, part, near, share,
+    near_send, near_recv,
     lift_send, lift_recv, gather_send, gather_recv, pass_send, pass_recv,
 ):
     section = lax.axis_index("section")
@@ -68,17 +70,16 @@
     def cut(j):
         return pl.ds(j * half, half)
 
-    def near_copy(which, t, j, k):
+    others = [(k, e) for k in range(chips) for e in range(2) if k + e > 0]
+    others = [pair_ for pair_ in others if pair_[0] > 0] + [(0, 1)]
+
+    def scatter_copy(which, t, p, k, e):
+        columns = pl.ds(pieces[which][p][0], pieces[which][p][1])
+        side = lax.rem(core + e, 2)
         return remote(
-            part.at[which, t, peer(k), 1 - core, :, cut(j)], near.at[which, t, k, :, cut(j)],
-            near_send.at[which, t, j, k], near_recv.at[which, t, j, k], {"head": twin},
-        )
-
-    def far_copy(which, t, j, k):
-        return remote(
-            away.at[which, t, k - 1, :, cut(j)], far.at[which, t, k - 1, :, cut(j)],
-            far_send.at[which, t, j, k - 1], far_recv.at[which, t, j, k - 1],
-            {"head": peer(k) * 2 + core},
+            part.at[which, t, peer(k), side, :, columns], near.at[which, t, k, e, :, columns],
+            near_send.at[which, t, p, k, e], near_recv.at[which, t, p, k, e],
+            {"head": peer(k) * 2 + side},
         )
 
     def lift_copy(which, t, j, target):
@@ -102,32 +103,21 @@
             pass_send.at[which, t, j, k], pass_recv.at[which, t, j, k], {"head": twin},
         )
 
-    def begin(which, t, j):
-        for k in list(range(1, chips)) + [0]:
-            near_copy(which, t, j, k).start()
-
-    def fold(which, t, j):
-        for k in range(1, chips):
-            near_copy(which, t, j, k).wait_recv()
-            away[which, t, k - 1, :, cut(j)] = (
-                part[which, t, peer(k), core, :, cut(j)].astype(F32)
-                + near[which, t, k, :, cut(j)].astype(F32)
-            ).astype(BF16)
-            far_copy(which, t, j, k).start()
+    def begin(which, t, p):
+        for k, e in others:
+            scatter_copy(which, t, p, k, e).start()
 
     def ends(which):
         if which == 0:
             return section < sections - 1, section + 1, section > 0, section - 1
         return section > 0, section - 1, section < sections - 1, section + 1
 
-    def reduced(which, t, j):
-        near_copy(which, t, j, 0).wait_recv()
-        own = part[which, t, chip, core, :, cut(j)].astype(F32) + near[
-            which, t, 0, :, cut(j)
-        ].astype(F32)
-        for k in range(1, chips):
-            far_copy(which, t, j, k).wait_recv()
-            own = own + far[which, t, k - 1, :, cut(j)].astype(F32)
+    def reduced(which, t, p):
+        columns = pl.ds(pieces[which][p][0], pieces[which][p][1])
+        own = part[which, t, chip, core, :, columns].astype(F32)
+        for k, e in others[::-1]:
+            scatter_copy(which, t, p, k, e).wait_recv()
+            own = own + near[which, t, k, e, :, columns].astype(F32)
         return own
 
     def hand_on(which, t, j, result):
@@ -155,7 +145,7 @@
         hand_on(0, t, j, (before + reduced(0, t, j)).astype(BF16))
 
     def finish_down(t):
-        own = jnp.concatenate([reduced(1, t, j) for j in range(halves)], axis=-1)
+        own = jnp.concatenate([reduced(1, t, p) for p in range(len(pieces[1]))], axis=-1)
         before = cur[1, t, chip, core].astype(F32)
         x = stash[t, chip, core].astype(F32)
         inverse = inverse_rms(x)
@@ -190,12 +180,13 @@
         for j in range(halves):
             for k in range(chips):
                 pass_copy(which, t, j, k).wait_recv()
+        for p in range(len(pieces[which])):
+            for k, e in others:
+                scatter_copy(which, t, p, k, e).wait_send()
         for j in range(halves):
             for k in range(chips):
-                near_copy(which, t, j, k).wait_send()
                 pass_copy(which, t, j, k).wait_send()
             for k in range(1, chips):
-                far_copy(which, t, j, k).wait_send()
                 gather_copy(which, t, j, k).wait_send()
             if t < last:
                 @pl.when(sends)
@@ -235,13 +226,16 @@
         for h in range(pair):
             acts[c][step * pair + h, at] = result[:, h * head_dim : (h + 1) * head_dim]
 
-    def project_pairs(place):
+    def project_pairs(place, hooks):
         def run(step, carry):
             project(0, step, place)
             project(1, step, place)
             return carry
 
-        lax.fori_loop(0, steps, run, 0)
+        lax.fori_loop(0, steps // 2, run, 0)
+        hooked(hooks, "mid")
+        lax.fori_loop(steps // 2, steps, run, 0)
+        hooked(hooks, "pairs")
 
     def block(emit):
         pl.when(section >= 0)(emit)
@@ -269,7 +263,7 @@
         for h in range(pair):
             probs[step * pair + h] = softmax(scores[h])
 
-    def out(t, hooks, base):
+    def out(t):
         for j in range(halves):
             each = half // lanes
             right = beside([wo[b] for b in range(j * each, (j + 1) * each)])
@@ -277,13 +271,11 @@
             result = mm(left, right, NN).astype(BF16)
             part[0, t, :, :, :, cut(j)] = result.reshape(part.shape[2:5] + (half,))
             begin(0, t, j)
-            hooked(hooks, base + j)
 
     def forward(t, hooks, also=None):
         count = 1 if also is None else 2
         if also is None:
-            project_pairs(0)
-            hooked(hooks, 0)
+            project_pairs(0, hooks)
 
         @functools.partial(block)
         def _():
@@ -296,12 +288,12 @@
                 blend(t, step, scores.pop(step))
                 if extra is not None:
                     keep(step, extra)
-                hooked(hooks, 2 + step)
-            out(t, hooks, 2 + steps)
+            hooked(hooks, "mixed")
+            out(t)
+        hooked(hooks, "end")
 
     def fill(place, hooks):
-        project_pairs(place)
-        hooked(hooks, 0)
+        project_pairs(place, hooks)
 
         @functools.partial(block)
         def _():
@@ -311,7 +303,7 @@
                 if step + 2 < steps:
                     scores[step + 2] = score(place, step + 2)
                 keep(step, scores.pop(step))
-        hooked(hooks, 1 + steps)
+        hooked(hooks, "end")
 
     def backward(t, hooks):
         place = t + 1
@@ -360,11 +352,12 @@
                     query_key_grads(step - 1)
                 hooked(hooks, step)
             query_key_grads(steps - 1)
-
-        for j in range(halves):
+        hooked(hooks, "steps")
+
+        for p, (low, size) in enumerate(pieces[1]):
             @functools.partial(block)
-            def _(j=j):
-                rows_of = slice(j * half, (j + 1) * half)
+            def _(p=p, low=low, size=size):
+                rows_of = slice(low, low + size)
                 back = [
                     mm(
                         beside([grads[c][n] for n in range(heads)]),
@@ -374,9 +367,11 @@
                     for c in (2, 0, 1)
                 ]
                 result = (back[0] + back[1] + back[2]).astype(BF16)
-                part[1, t, :, :, :, cut(j)] = result.reshape(part.shape[2:5] + (half,))
-                begin(1, t, j)
-                hooked(hooks, steps + j)
+                part[1, t, :, :, :, pl.ds(low, size)] = result.reshape(
+                    part.shape[2:5] + (size,)
+                )
+                begin(1, t, p)
+            hooked(hooks, f"back{p}")
 
     def tables(low, high):
         def run(b, carry):
@@ -397,10 +392,21 @@
             wo_hbm.at[:, pl.ds(b * lanes, lanes)], wo.at[b], wo_sem.at[b]
         )
 
+    small = [
+        pltpu.make_async_copy(source, target, in_sem.at[n])
+        for n, (source, target) in enumerate((
+            (labels_hbm, labels), (buckets_hbm, buckets), (gain_hbm, gain),
+            (rising, cur.at[0, 0]), (falling, cur.at[1, 0]),
+            (stash_hbm, stash), (queue_hbm, queue),
+        ))
+    ]
+    for copy in small[:-1]:
+        copy.start()
     fetch(0).start()
+    small[-1].start()
     fetch(1).start()
     barrier = pltpu.get_barrier_semaphore()
-    greeted = [twin] + [peer(k) * 2 + core for k in range(1, chips)]
+    greeted = [peer(k) * 2 + lax.rem(core + e, 2) for k, e in others]
     for other in greeted:
         pl.semaphore_signal(barrier, inc=1, device_id={"head": other}, device_id_type=MESH)
 
@@ -416,16 +422,18 @@
             barrier, inc=1, device_id={"section": section + 1}, device_id_type=MESH
         )
 
+    small[0].wait()
+    small[1].wait()
     blank = jnp.zeros((heads, lanes - labels.shape[1]), F32)
     lookup = jnp.concatenate([labels[...], blank], axis=1)
     for n in range(heads):
         bias[n] = jnp.take_along_axis(
             jnp.broadcast_to(lookup[n : n + 1], (rows, lanes)), buckets[...], axis=1
         )
-    cur[0, 0] = rising[...]
-    cur[1, 0] = falling[...]
-    lower(flat(falling[...]))
-    normalize(0, flat(rising[...]))
+    for copy in small[2:]:
+        copy.wait()
+    lower(flat(cur[1, 0]))
+    normalize(0, flat(cur[0, 0]))
     for t in range(ticks):
         normalize(t + 1, flat(stash[t]))
 
@@ -465,42 +473,33 @@
     def both(function, which, t):
         return [do(function, which, t, j) for j in range(halves)]
 
-    s = steps
     forward(0, {}, also=1)
     for t in range(ticks):
         backward(t, {
-            0: both(fold, 0, t),
-            s - 1 if s > 1 else 1: [do(finish_up, t, 0)],
-            s: [do(finish_up, t, j) for j in range(1, halves)],
-            s + halves - 1: both(spread, 0, t),
+            max(steps - 2, 0): [do(finish_up, t, 0)],
+            "steps": [do(finish_up, t, j) for j in range(1, halves)],
+            f"back{len(pieces[1]) - 2}": [do(spread, 0, t, 0)],
+            f"back{len(pieces[1]) - 1}": [do(spread, 0, t, j) for j in range(1, halves)],
         })
         if t < last:
-            fill(t + 2, {
-                0: both(fold, 1, t),
-                1 + s: [do(finish_down, t)] + both(relay, 0, t),
-            })
+            fill(t + 2, {"pairs": [do(finish_down, t)] + both(relay, 0, t)})
             settle(0, t)
             normalize(0, flat(cur[0, t + 1]))
-            forward(t + 1, {
-                2: both(spread, 1, t),
-                1 + s + halves: both(relay, 1, t),
-            })
+            forward(t + 1, {"mid": both(spread, 1, t), "mixed": both(relay, 1, t)})
             settle(1, t)
             lower(flat(cur[1, t + 1]))
     count = sums.shape[0]
-    tables(0, count // 5)
-    for action in both(fold, 1, last) + both(relay, 0, last):
+    tables(0, count * 2 // 5)
+    finish_down(last)
+    for action in both(spread, 1, last) + both(relay, 0, last):
         action()
     settle(0, last)
     moved[0] = cur[0, ticks]
-    tables(count // 5, count * 7 // 10)
-    finish_down(last)
-    for action in both(spread, 1, last):
-        action()
-    tables(count * 7 // 10, count)
-    table[...] = jnp.sum(sums[...], axis=-1)
+    tables(count * 2 // 5, count * 4 // 5)
     for action in both(relay, 1, last):
         action()
+    tables(count * 4 // 5, count)
+    table[...] = jnp.sum(sums[...], axis=-1)
     settle(1, last)
     moved[1] = cur[1, ticks]
 
@@ -515,6 +514,11 @@
     pair = next(p for p in (4, 2, 1) if heads % p == 0)
     others = max(chips - 1, 1)
     halves, group, lanes = 2, 16, 128
+    half, quarter = width // 2, width // 4
+    pieces = (
+        ((0, half), (half, half)),
+        ((0, half), (half, quarter), (half + quarter, quarter)),
+    )
     flat_heads = heads * head_dim
     w_in = jnp.swapaxes(w_qkv[0], 1, 2)
     w_back = w_out[0].reshape(flat_heads, width)
@@ -526,15 +530,21 @@
     dma = lambda *shape: pltpu.SemaphoreType.DMA(shape)
     moved, table = pl.pallas_call(
         functools.partial(
-            wave_kernel, ticks, pair, head_dim, chips, sections, halves, group
+            wave_kernel, ticks, pair, head_dim, chips, sections, halves, pieces, group
         ),
-        in_specs=[pl.BlockSpec(memory_space=pltpu.SMEM)] + [vmem] * 7 + [pl.BlockSpec(memory_space=pl.ANY)] * 2,
+        in_specs=[pl.BlockSpec(memory_space=pltpu.SMEM)] + [pl.BlockSpec(memory_space=pltpu.HBM)] * 9,
         out_specs=[vmem] * 2,
         out_shape=[
             jax.ShapeDtypeStruct((2, chips, 2) + tile, BF16),
             jax.ShapeDtypeStruct((bias_table.shape[1], heads), F32),
         ],
         scratch_shapes=[
+            bf16(ticks, chips, 2, *tile),
+            bf16(queue.shape[0], chips, 2, *tile),
+            f32(1, width),
+            f32(heads, bias_table.shape[1]),
+            pltpu.VMEM(buckets.shape, jnp.int32),
+            dma(7),
             f32(heads, rows, rows),
             bf16(2, width, heads, head_dim),
             dma(3),
@@ -559,18 +569,15 @@
             f32(bias_table.shape[1], heads, rows),
             bf16(2, ticks + 1, chips, 2, *tile),
             bf16(2, ticks, chips, 2, *tile),
-            bf16(2, ticks, chips, *tile),
-            bf16(2, ticks, others, *tile),
-            bf16(2, ticks, others, *tile),
+            bf16(2, ticks, chips, 2, *tile),
             bf16(2, ticks, *tile),
-            dma(2, ticks, halves, chips), dma(2, ticks, halves, chips),
-            dma(2, ticks, halves, others), dma(2, ticks, halves, others),
+            dma(2, ticks, 3, chips, 2), dma(2, ticks, 3, chips, 2),
             dma(2, ticks, halves), dma(2, ticks, halves),
             dma(2, ticks, halves, others), dma(2, ticks, halves, others),
             dma(2, ticks, halves, chips), dma(2, ticks, halves, chips),
         ],
         compiler_params=pltpu.CompilerParams(
-            collective_id=0, has_side_effects=True, vmem_limit_bytes=52 << 20
+            collective_id=0, has_side_effects=True, vmem_limit_bytes=58 << 20
         ),
     )(
         order, split(rising[0]), split(falling[0]), split(stash[0]), split(queue), gain,

time: 88.6 us -> 81.2 us (0.916)
  local copies, waits for them, and re-layouts: 7.41 us -> 3.24 us
  Pallas kernels: 80.2 us -> 77 us
    unnamed x15 -> x1, local copies, waits for them, and re-layouts: 6.57 us -> 1.39 us
    pallas_call x1, Pallas kernels: 80.2 us -> 77 us  [per_device(): pl.pallas_call(functools.partial(wave_kernel, ticks, pair, head_dim, chip...]
    slice x1, local copies, waits for them, and re-layouts: 0.84 us -> 1.85 us  [per_device(): return (moved[0], moved[1], table[None])]
where the time goes in v2:
time: 81.2 us; the launch traced here: 80.9 us
  Pallas kernels  77 us (95%)
  local copies, waits for them, and re-layouts  3.24 us (4%)
    pallas_call x1, Pallas kernels, per_device(): pl.pallas_call(functools.partial(wave_kernel, ticks, pair, head_dim, chip...  77 us
    slice x1, local copies, waits for them, and re-layouts, per_device(): return (moved[0], moved[1], table[None])  1.85 us

profile of v2, /device:TPU:0, one launch (start us, length us, event | category | flops | bytes accessed | tf_op | source)
XLA Modules:
  0.0 80.9 jit_solution(14292564890303262861)
XLA Ops:
  0.6 77.0 %shard_map.121 = (bf16[2,2,2,32,1024]{4,3,2,1,0:T(8,128)(2,1)}, f32[32,16]{1,0:T(8,128)}) custom-call(s32[6]{0:T(128)} %order.1, bf16[2,2,32,1024]{3,2,1,0:T(8,128)(2,1)} %bitcast.18, bf16[2,2,32,1024]{3,2,1,0:T(8,128)(2,1)} %bitcast.19, bf16[3,2,2,32,1024]{4,3,2,1,0:T(8,128)(2,1)} %bitcast.17, bf16[6,2,2,32,1024]{4,3,2,1,0:T(8,128)(2,1)} %bitcast.16, ...), custom_call_target="tpu_custom_call" | custom-call | tf_op jit(solution)/shard_map/pallas_call | solution.py:531
  77.7 1.4 %copy.13 = f32[1,32,16]{1,2,0:T(8,128)} copy(f32[1,32,16]{2,1,0:T(8,128)} %bitcast.22) | data formatting | bytes 4096
  79.1 1.9 %fusion = (bf16[1,2,2,32,1024]{4,3,2,1,0:T(8,128)(2,1)}, bf16[1,2,2,32,1024]{4,3,2,1,0:T(8,128)(2,1)}) fusion(bf16[2,2,2,32,1024]{4,3,2,1,0:T(8,128)(2,1)} %get-tuple-element.5), kind=kLoop, calls=%fused_computation | loop fusion | bytes 1048576 | tf_op jit(solution)/shard_map/slice | solution.py:587

commit v3 on v2

--- a/solution.py
+++ b/solution.py
@@ -37,9 +37,9 @@
     stash, queue, gain, labels, buckets, in_sem,
     bias, raw, w_sem, wo, wo_sem, wq, wk, wv, aq, ak, av, normed, probs, attended,
     gflat, gq, gk, gv, thin, flat_down, total, sums,
-    cur, part, near, share,
-    near_send, near_recv,
-    lift_send, lift_recv, gather_send, gather_recv, pass_send, pass_recv,
+    cur, part, near, far, share,
+    near_send, near_recv, far_send, far_recv,
+    lift_send, lift_recv, pass_send, pass_recv,
 ):
     section = lax.axis_index("section")
     head = lax.axis_index("head")
@@ -70,42 +70,48 @@
     def cut(j):
         return pl.ds(j * half, half)
 
-    others = [(k, e) for k in range(chips) for e in range(2) if k + e > 0]
-    others = [pair_ for pair_ in others if pair_[0] > 0] + [(0, 1)]
-
-    def scatter_copy(which, t, p, k, e):
-        columns = pl.ds(pieces[which][p][0], pieces[which][p][1])
-        side = lax.rem(core + e, 2)
+    def piece(which, p):
+        return pl.ds(pieces[which][p][0], pieces[which][p][1])
+
+    def near_copy(which, t, p):
         return remote(
-            part.at[which, t, peer(k), side, :, columns], near.at[which, t, k, e, :, columns],
-            near_send.at[which, t, p, k, e], near_recv.at[which, t, p, k, e],
-            {"head": peer(k) * 2 + side},
+            part.at[which, t, 1 - core, :, piece(which, p)],
+            near.at[which, t, :, piece(which, p)],
+            near_send.at[which, t, p], near_recv.at[which, t, p], {"head": twin},
+        )
+
+    def far_copy(which, t, p, k):
+        rows_here = far.at[which, t, chip, :, piece(which, p)]
+        return remote(
+            rows_here, rows_here,
+            far_send.at[which, t, p, k - 1], far_recv.at[which, t, p, k - 1],
+            {"head": peer(k) * 2 + core},
         )
 
     def lift_copy(which, t, j, target):
         return remote(
-            share.at[which, t, :, cut(j)], cur.at[which, t + 1, chip, core, :, cut(j)],
+            share.at[which, t, :, cut(j)], cur.at[which, t + 1, core, :, cut(j)],
             lift_send.at[which, t, j], lift_recv.at[which, t, j], {"section": target},
         )
 
-    def gather_copy(which, t, j, k):
-        rows_here = cur.at[which, t + 1, chip, core, :, cut(j)]
+    def pass_copy(which, t, j):
+        rows_here = cur.at[which, t + 1, core, :, cut(j)]
         return remote(
             rows_here, rows_here,
-            gather_send.at[which, t, j, k - 1], gather_recv.at[which, t, j, k - 1],
-            {"head": peer(k) * 2 + core},
-        )
-
-    def pass_copy(which, t, j, k):
-        rows_here = cur.at[which, t + 1, lax.rem(chip - k + chips, chips), core, :, cut(j)]
-        return remote(
-            rows_here, rows_here,
-            pass_send.at[which, t, j, k], pass_recv.at[which, t, j, k], {"head": twin},
+            pass_send.at[which, t, j], pass_recv.at[which, t, j], {"head": twin},
         )
 
     def begin(which, t, p):
-        for k, e in others:
-            scatter_copy(which, t, p, k, e).start()
+        near_copy(which, t, p).start()
+
+    def fold(which, t, p):
+        near_copy(which, t, p).wait_recv()
+        far[which, t, chip, :, piece(which, p)] = (
+            part[which, t, core, :, piece(which, p)].astype(F32)
+            + near[which, t, :, piece(which, p)].astype(F32)
+        ).astype(BF16)
+        for k in range(1, chips):
+            far_copy(which, t, p, k).start()
 
     def ends(which):
         if which == 0:
@@ -113,17 +119,17 @@
         return section > 0, section - 1, section < sections - 1, section + 1
 
     def reduced(which, t, p):
-        columns = pl.ds(pieces[which][p][0], pieces[which][p][1])
-        own = part[which, t, chip, core, :, columns].astype(F32)
-        for k, e in others[::-1]:
-            scatter_copy(which, t, p, k, e).wait_recv()
-            own = own + near[which, t, k, e, :, columns].astype(F32)
+        for k in range(1, chips):
+            far_copy(which, t, p, k).wait_recv()
+        own = far[which, t, 0, :, piece(which, p)].astype(F32)
+        for c in range(1, chips):
+            own = own + far[which, t, c, :, piece(which, p)].astype(F32)
         return own
 
     def hand_on(which, t, j, result):
         sends, target, receives, _ = ends(which)
         if t == last:
-            cur[which, t + 1, chip, core, :, cut(j)] = result
+            cur[which, t + 1, core, :, cut(j)] = result
             return
         share[which, t, :, cut(j)] = result
 
@@ -134,20 +140,18 @@
         @pl.when(jnp.logical_not(receives))
         def _():
             if which == 0:
-                cur[which, t + 1, chip, core, :, cut(j)] = queue[
-                    order[t], chip, core, :, cut(j)
-                ]
+                cur[which, t + 1, core, :, cut(j)] = queue[order[t], core, :, cut(j)]
             else:
-                cur[which, t + 1, chip, core, :, cut(j)] = share[0, t, :, cut(j)]
+                cur[which, t + 1, core, :, cut(j)] = share[0, t, :, cut(j)]
 
     def finish_up(t, j):
-        before = cur[0, t, chip, core, :, cut(j)].astype(F32)
+        before = cur[0, t, core, :, cut(j)].astype(F32)
         hand_on(0, t, j, (before + reduced(0, t, j)).astype(BF16))
 
     def finish_down(t):
         own = jnp.concatenate([reduced(1, t, p) for p in range(len(pieces[1]))], axis=-1)
-        before = cur[1, t, chip, core].astype(F32)
-        x = stash[t, chip, core].astype(F32)
+        before = cur[1, t, core].astype(F32)
+        x = stash[t, core].astype(F32)
         inverse = inverse_rms(x)
         cubed = inverse * inverse * inverse
         weighted = gain[...] * own
@@ -159,35 +163,25 @@
         for j in range(halves):
             hand_on(1, t, j, result[:, j * half : (j + 1) * half])
 
-    def spread(which, t, j):
+    def relay(which, t, j):
         _, _, receives, source = ends(which)
         if t < last:
             @pl.when(receives)
             def _():
                 lift_copy(which, t, j, source).wait_recv()
 
-        for k in range(1, chips):
-            gather_copy(which, t, j, k).start()
-        pass_copy(which, t, j, 0).start()
-
-    def relay(which, t, j):
-        for k in range(1, chips):
-            gather_copy(which, t, j, k).wait_recv()
-            pass_copy(which, t, j, k).start()
+        pass_copy(which, t, j).start()
 
     def settle(which, t):
         sends, target, _, _ = ends(which)
         for j in range(halves):
-            for k in range(chips):
-                pass_copy(which, t, j, k).wait_recv()
+            pass_copy(which, t, j).wait_recv()
         for p in range(len(pieces[which])):
-            for k, e in others:
-                scatter_copy(which, t, p, k, e).wait_send()
+            near_copy(which, t, p).wait_send()
+            for k in range(1, chips):
+                far_copy(which, t, p, k).wait_send()
         for j in range(halves):
-            for k in range(chips):
-                pass_copy(which, t, j, k).wait_send()
-            for k in range(1, chips):
-                gather_copy(which, t, j, k).wait_send()
+            pass_copy(which, t, j).wait_send()
             if t < last:
                 @pl.when(sends)
                 def _(j=j):
@@ -269,7 +263,7 @@
             right = beside([wo[b] for b in range(j * each, (j + 1) * each)])
             left = beside([attended[n] for n in range(heads)])
             result = mm(left, right, NN).astype(BF16)
-            part[0, t, :, :, :, cut(j)] = result.reshape(part.shape[2:5] + (half,))
+            part[0, t, :, :, cut(j)] = result.reshape(part.shape[2:4] + (half,))
             begin(0, t, j)
 
     def forward(t, hooks, also=None):
@@ -288,7 +282,7 @@
                 blend(t, step, scores.pop(step))
                 if extra is not None:
                     keep(step, extra)
-            hooked(hooks, "mixed")
+                hooked(hooks, step)
             out(t)
         hooked(hooks, "end")
 
@@ -303,6 +297,7 @@
                 if step + 2 < steps:
                     scores[step + 2] = score(place, step + 2)
                 keep(step, scores.pop(step))
+                hooked(hooks, step)
         hooked(hooks, "end")
 
     def backward(t, hooks):
@@ -358,17 +353,16 @@
             @functools.partial(block)
             def _(p=p, low=low, size=size):
                 rows_of = slice(low, low + size)
-                back = [
-                    mm(
+                back = []
+                for c in (2, 0, 1):
+                    back.append(mm(
                         beside([grads[c][n] for n in range(heads)]),
                         beside([weights[c][n, rows_of] for n in range(heads)]),
                         NT,
-                    )
-                    for c in (2, 0, 1)
-                ]
+                    ))
                 result = (back[0] + back[1] + back[2]).astype(BF16)
-                part[1, t, :, :, :, pl.ds(low, size)] = result.reshape(
-                    part.shape[2:5] + (size,)
+                part[1, t, :, :, pl.ds(low, size)] = result.reshape(
+                    part.shape[2:4] + (size,)
                 )
                 begin(1, t, p)
             hooked(hooks, f"back{p}")
@@ -406,7 +400,7 @@
     small[-1].start()
     fetch(1).start()
     barrier = pltpu.get_barrier_semaphore()
-    greeted = [peer(k) * 2 + lax.rem(core + e, 2) for k, e in others]
+    greeted = [twin] + [peer(k) * 2 + core for k in range(1, chips)]
     for other in greeted:
         pl.semaphore_signal(barrier, inc=1, device_id={"head": other}, device_id_type=MESH)
 
@@ -475,30 +469,41 @@
 
     forward(0, {}, also=1)
     for t in range(ticks):
+        down = range(len(pieces[1]))
         backward(t, {
-            max(steps - 2, 0): [do(finish_up, t, 0)],
-            "steps": [do(finish_up, t, j) for j in range(1, halves)],
-            f"back{len(pieces[1]) - 2}": [do(spread, 0, t, 0)],
-            f"back{len(pieces[1]) - 1}": [do(spread, 0, t, j) for j in range(1, halves)],
+            0: both(fold, 0, t),
+            "steps": [do(finish_up, t, 0)],
+            "back0": [do(finish_up, t, j) for j in range(1, halves)],
+            f"back{down[-2]}": [do(fold, 1, t, p) for p in down[:-2]],
+            f"back{down[-1]}": [do(fold, 1, t, p) for p in down[-2:-1]] + [do(relay, 0, t, 0)],
         })
         if t < last:
-            fill(t + 2, {"pairs": [do(finish_down, t)] + both(relay, 0, t)})
+            final = do(fold, 1, t, down[-1])
+            others = [do(relay, 0, t, j) for j in range(1, halves)]
+            middle = min(1, steps - 1)
+            fill(t + 2, {
+                "mid": [final], "pairs": others, max(steps - 2, 0): [do(finish_down, t)],
+            })
             settle(0, t)
             normalize(0, flat(cur[0, t + 1]))
-            forward(t + 1, {"mid": both(spread, 1, t), "mixed": both(relay, 1, t)})
+            forward(t + 1, {
+                "pairs": [do(relay, 1, t, 0)],
+                middle: [do(relay, 1, t, j) for j in range(1, halves)],
+            })
             settle(1, t)
             lower(flat(cur[1, t + 1]))
     count = sums.shape[0]
-    tables(0, count * 2 // 5)
-    finish_down(last)
-    for action in both(spread, 1, last) + both(relay, 0, last):
-        action()
+    tables(0, count // 5)
+    fold(1, last, len(pieces[1]) - 1)
+    for j in range(1, halves):
+        relay(0, last, j)
+    tables(count // 5, count * 3 // 5)
     settle(0, last)
     moved[0] = cur[0, ticks]
-    tables(count * 2 // 5, count * 4 // 5)
-    for action in both(relay, 1, last):
-        action()
-    tables(count * 4 // 5, count)
+    finish_down(last)
+    for j in range(halves):
+        relay(1, last, j)
+    tables(count * 3 // 5, count)
     table[...] = jnp.sum(sums[...], axis=-1)
     settle(1, last)
     moved[1] = cur[1, ticks]
@@ -510,7 +515,7 @@
     ticks = stash.shape[1]
     rows, width = rising.shape[1:]
     heads, head_dim = w_qkv.shape[2], w_qkv.shape[4]
-    chips, part_rows = head_count // 2, rows // head_count
+    chips = head_count // 2
     pair = next(p for p in (4, 2, 1) if heads % p == 0)
     others = max(chips - 1, 1)
     halves, group, lanes = 2, 16, 128
@@ -522,9 +527,9 @@
     flat_heads = heads * head_dim
     w_in = jnp.swapaxes(w_qkv[0], 1, 2)
     w_back = w_out[0].reshape(flat_heads, width)
-    split = lambda a: a.reshape(a.shape[:-2] + (chips, 2, part_rows, width))
+    split = lambda a: a.reshape(a.shape[:-2] + (2, rows // 2, width))
     vmem = pl.BlockSpec(memory_space=pltpu.VMEM)
-    tile = (part_rows, width)
+    tile = (rows // 2, width)
     bf16 = lambda *shape: pltpu.VMEM(shape, BF16)
     f32 = lambda *shape: pltpu.VMEM(shape, F32)
     dma = lambda *shape: pltpu.SemaphoreType.DMA(shape)
@@ -535,12 +540,12 @@
         in_specs=[pl.BlockSpec(memory_space=pltpu.SMEM)] + [pl.BlockSpec(memory_space=pltpu.HBM)] * 9,
         out_specs=[vmem] * 2,
         out_shape=[
-            jax.ShapeDtypeStruct((2, chips, 2) + tile, BF16),
+            jax.ShapeDtypeStruct((2, 2) + tile, BF16),
             jax.ShapeDtypeStruct((bias_table.shape[1], heads), F32),
         ],
         scratch_shapes=[
-            bf16(ticks, chips, 2, *tile),
-            bf16(queue.shape[0], chips, 2, *tile),
+            bf16(ticks, 2, *tile),
+            bf16(queue.shape[0], 2, *tile),
             f32(1, width),
             f32(heads, bias_table.shape[1]),
             pltpu.VMEM(buckets.shape, jnp.int32),
@@ -567,17 +572,18 @@
             bf16(width // lanes, rows, lanes),
             f32(heads, rows, rows),
             f32(bias_table.shape[1], heads, rows),
-            bf16(2, ticks + 1, chips, 2, *tile),
-            bf16(2, ticks, chips, 2, *tile),
-            bf16(2, ticks, chips, 2, *tile),
+            bf16(2, ticks + 1, 2, *tile),
+            bf16(2, ticks, 2, *tile),
             bf16(2, ticks, *tile),
-            dma(2, ticks, 3, chips, 2), dma(2, ticks, 3, chips, 2),
+            bf16(2, ticks, chips, *tile),
+            bf16(2, ticks, *tile),
+            dma(2, ticks, 3), dma(2, ticks, 3),
+            dma(2, ticks, 3, others), dma(2, ticks, 3, others),
             dma(2, ticks, halves), dma(2, ticks, halves),
-            dma(2, ticks, halves, others), dma(2, ticks, halves, others),
-            dma(2, ticks, halves, chips), dma(2, ticks, halves, chips),
+            dma(2, ticks, halves), dma(2, ticks, halves),
         ],
         compiler_params=pltpu.CompilerParams(
-            collective_id=0, has_side_effects=True, vmem_limit_bytes=58 << 20
+            collective_id=0, has_side_effects=True, vmem_limit_bytes=54 << 20
         ),
     )(
         order, split(rising[0]), split(falling[0]), split(stash[0]), split(queue), gain,

time: 81.2 us -> 77.6 us (0.956)
  Pallas kernels: 77 us -> 73.4 us
    pallas_call x1, Pallas kernels: 77 us -> 73.4 us  [per_device(): pl.pallas_call(functools.partial(wave_kernel, ticks, pair, head_dim, chip...]
where the time goes in v3:
time: 77.6 us; the launch traced here: 77.2 us
  Pallas kernels  73.4 us (95%)
  local copies, waits for them, and re-layouts  3.24 us (4%)
    pallas_call x1, Pallas kernels, per_device(): pl.pallas_call(functools.partial(wave_kernel, ticks, pair, head_dim, chip...  73.4 us
    slice x1, local copies, waits for them, and re-layouts, per_device(): return (moved[0], moved[1], table[None])  1.85 us

profile of v3, /device:TPU:0, one launch (start us, length us, event | category | flops | bytes accessed | tf_op | source)
XLA Modules:
  0.0 77.2 jit_solution(9763186701157306564)
XLA Ops:
  0.6 73.4 %shard_map.121 = (bf16[2,2,64,1024]{3,2,1,0:T(8,128)(2,1)}, f32[32,16]{1,0:T(8,128)}) custom-call(s32[6]{0:T(128)} %order.1, bf16[2,64,1024]{2,1,0:T(8,128)(2,1)} %bitcast.18, bf16[2,64,1024]{2,1,0:T(8,128)(2,1)} %bitcast.19, bf16[3,2,64,1024]{3,2,1,0:T(8,128)(2,1)} %bitcast.17, bf16[6,2,64,1024]{3,2,1,0:T(8,128)(2,1)} %bitcast.16, f32[1,1024]{1,0:T(1,128)} %gain_hbm.1, ...), custom_call_target="tpu_custom_call" | custom-call | tf_op jit(solution)/shard_map/pallas_call | solution.py:536
  74.0 1.4 %copy.13 = f32[1,32,16]{1,2,0:T(8,128)} copy(f32[1,32,16]{2,1,0:T(8,128)} %bitcast.22) | data formatting | bytes 4096
  75.4 1.9 %fusion = (bf16[1,2,64,1024]{3,2,1,0:T(8,128)(2,1)}, bf16[1,2,64,1024]{3,2,1,0:T(8,128)(2,1)}) fusion(bf16[2,2,64,1024]{3,2,1,0:T(8,128)(2,1)} %get-tuple-element.5), kind=kLoop, calls=%fused_computation | loop fusion | bytes 1048576 | tf_op jit(solution)/shard_map/slice | solution.py:593

commit v4 on v3

--- a/solution.py
+++ b/solution.py
@@ -221,14 +221,11 @@
             acts[c][step * pair + h, at] = result[:, h * head_dim : (h + 1) * head_dim]
 
     def project_pairs(place, hooks):
-        def run(step, carry):
+        for step in range(steps):
+            if step == steps // 2:
+                hooked(hooks, "mid")
             project(0, step, place)
             project(1, step, place)
-            return carry
-
-        lax.fori_loop(0, steps // 2, run, 0)
-        hooked(hooks, "mid")
-        lax.fori_loop(steps // 2, steps, run, 0)
         hooked(hooks, "pairs")
 
     def block(emit):
@@ -446,12 +443,16 @@
     for c in (1, 2):
         fetch(c).wait()
 
-        def under(step, carry, c=c):
-            project(c - 1, step, 0, 2)
-            relay_weights(c, step * (blocks // steps), blocks // steps)
+        stride = 2 if steps % 2 == 0 else 1
+
+        def under(turn, carry, c=c):
+            for n in range(stride):
+                step = turn * stride + n
+                project(c - 1, step, 0, 2)
+                relay_weights(c, step * (blocks // steps), blocks // steps)
             return carry
 
-        lax.fori_loop(0, steps, under, 0)
+        lax.fori_loop(0, steps // stride, under, 0)
     for b in range(tiles):
         fetch_out(b).wait()
     pl.semaphore_wait(

time: 77.6 us -> 77.7 us (level)
  no operation moved by 1% of the time
where the time goes in v4:
time: 77.7 us; the launch traced here: 77.3 us
  Pallas kernels  73.5 us (95%)
  local copies, waits for them, and re-layouts  3.24 us (4%)
    pallas_call x1, Pallas kernels, per_device(): pl.pallas_call(functools.partial(wave_kernel, ticks, pair, head_dim, chip...  73.5 us
    slice x1, local copies, waits for them, and re-layouts, per_device(): return (moved[0], moved[1], table[None])  1.85 us

profile of v4, /device:TPU:0, one launch (start us, length us, event | category | flops | bytes accessed | tf_op | source)
XLA Modules:
  0.0 77.3 jit_solution(12656476626012593374)
XLA Ops:
  0.6 73.5 %shard_map.121 = (bf16[2,2,64,1024]{3,2,1,0:T(8,128)(2,1)}, f32[32,16]{1,0:T(8,128)}) custom-call(s32[6]{0:T(128)} %order.1, bf16[2,64,1024]{2,1,0:T(8,128)(2,1)} %bitcast.18, bf16[2,64,1024]{2,1,0:T(8,128)(2,1)} %bitcast.19, bf16[3,2,64,1024]{3,2,1,0:T(8,128)(2,1)} %bitcast.17, bf16[6,2,64,1024]{3,2,1,0:T(8,128)(2,1)} %bitcast.16, f32[1,1024]{1,0:T(1,128)} %gain_hbm.1, ...), custom_call_target="tpu_custom_call" | custom-call | tf_op jit(solution)/shard_map/pallas_call | solution.py:537
  74.1 1.4 %copy.13 = f32[1,32,16]{1,2,0:T(8,128)} copy(f32[1,32,16]{2,1,0:T(8,128)} %bitcast.22) | data formatting | bytes 4096
  75.5 1.9 %fusion = (bf16[1,2,64,1024]{3,2,1,0:T(8,128)(2,1)}, bf16[1,2,64,1024]{3,2,1,0:T(8,128)(2,1)}) fusion(bf16[2,2,64,1024]{3,2,1,0:T(8,128)(2,1)} %get-tuple-element.5), kind=kLoop, calls=%fused_computation | loop fusion | bytes 1048576 | tf_op jit(solution)/shard_map/slice | solution.py:594

commit v5 on v4

--- a/solution.py
+++ b/solution.py
@@ -471,32 +471,28 @@
     forward(0, {}, also=1)
     for t in range(ticks):
         down = range(len(pieces[1]))
+        tail = [do(fold, 1, t, down[-2])]
         backward(t, {
-            0: both(fold, 0, t),
-            "steps": [do(finish_up, t, 0)],
-            "back0": [do(finish_up, t, j) for j in range(1, halves)],
-            f"back{down[-2]}": [do(fold, 1, t, p) for p in down[:-2]],
-            f"back{down[-1]}": [do(fold, 1, t, p) for p in down[-2:-1]] + [do(relay, 0, t, 0)],
+            min(1, steps - 1): both(fold, 0, t),
+            "back0": [do(finish_up, t, 0)],
+            f"back{down[-2]}": [do(finish_up, t, j) for j in range(1, halves)]
+            + [do(fold, 1, t, p) for p in down[:-2]],
+            f"back{down[-1]}": tail if t == last else [],
         })
         if t < last:
-            final = do(fold, 1, t, down[-1])
-            others = [do(relay, 0, t, j) for j in range(1, halves)]
-            middle = min(1, steps - 1)
+            final = [do(fold, 1, t, down[-1])]
             fill(t + 2, {
-                "mid": [final], "pairs": others, max(steps - 2, 0): [do(finish_down, t)],
+                "mid": tail + final, "pairs": both(relay, 0, t), "end": [do(finish_down, t)],
             })
             settle(0, t)
             normalize(0, flat(cur[0, t + 1]))
-            forward(t + 1, {
-                "pairs": [do(relay, 1, t, 0)],
-                middle: [do(relay, 1, t, j) for j in range(1, halves)],
-            })
+            forward(t + 1, {steps - 1: both(relay, 1, t)})
             settle(1, t)
             lower(flat(cur[1, t + 1]))
     count = sums.shape[0]
     tables(0, count // 5)
     fold(1, last, len(pieces[1]) - 1)
-    for j in range(1, halves):
+    for j in range(halves):
         relay(0, last, j)
     tables(count // 5, count * 3 // 5)
     settle(0, last)

time: 77.7 us -> 71.7 us (0.923)
  Pallas kernels: 73.5 us -> 67.5 us
    pallas_call x1, Pallas kernels: 73.5 us -> 67.5 us  [per_device(): pl.pallas_call(functools.partial(wave_kernel, ticks, pair, head_dim, chip...]
where the time goes in v5:
time: 71.7 us; the launch traced here: 71.4 us
  Pallas kernels  67.5 us (94%)
  local copies, waits for them, and re-layouts  3.24 us (5%)
    pallas_call x1, Pallas kernels, per_device(): pl.pallas_call(functools.partial(wave_kernel, ticks, pair, head_dim, chip...  67.5 us
    slice x1, local copies, waits for them, and re-layouts, per_device(): return (moved[0], moved[1], table[None])  1.85 us

profile of v5, /device:TPU:0, one launch (start us, length us, event | category | flops | bytes accessed | tf_op | source)
XLA Modules:
  0.0 71.4 jit_solution(15841138115853256182)
XLA Ops:
  0.6 67.5 %shard_map.121 = (bf16[2,2,64,1024]{3,2,1,0:T(8,128)(2,1)}, f32[32,16]{1,0:T(8,128)}) custom-call(s32[6]{0:T(128)} %order.1, bf16[2,64,1024]{2,1,0:T(8,128)(2,1)} %bitcast.18, bf16[2,64,1024]{2,1,0:T(8,128)(2,1)} %bitcast.19, bf16[3,2,64,1024]{3,2,1,0:T(8,128)(2,1)} %bitcast.17, bf16[6,2,64,1024]{3,2,1,0:T(8,128)(2,1)} %bitcast.16, f32[1,1024]{1,0:T(1,128)} %gain_hbm.1, ...), custom_call_target="tpu_custom_call" | custom-call | tf_op jit(solution)/shard_map/pallas_call | solution.py:533
  68.1 1.4 %copy.13 = f32[1,32,16]{1,2,0:T(8,128)} copy(f32[1,32,16]{2,1,0:T(8,128)} %bitcast.22) | data formatting | bytes 4096
  69.5 1.9 %fusion = (bf16[1,2,64,1024]{3,2,1,0:T(8,128)(2,1)}, bf16[1,2,64,1024]{3,2,1,0:T(8,128)(2,1)}) fusion(bf16[2,2,64,1024]{3,2,1,0:T(8,128)(2,1)} %get-tuple-element.5), kind=kLoop, calls=%fused_computation | loop fusion | bytes 1048576 | tf_op jit(solution)/shard_map/slice | solution.py:590
